TPU v7x, 128 devices: a whole 4x4x4 slice. The times are simulated.
128 devices in a mesh: inst: 32 (over x, y, core), arch: 4 (over z).
Axes of the slice: x: 4, y: 4, z: 4, core: 2. Of those that a mesh axis runs over, the one named last changes fastest.
Arguments:
- instance_arch: int32 [8192], P(('inst', 'arch')), may hold values from 0 to 39
- instance_param: int32 [8192], P(('inst', 'arch')), may hold values from 0 to 1023
- instance_ports: int32 [8192, 4], P(('inst', 'arch')), may hold values from 0 to 16383, as said below
- port_row: int32 [16384], replicated, may hold values from 0 to 16383, as said below
- param_table: float32 [1024, 64], replicated, may hold values from 0.5 to 2
- bubble_inverse: float32 [40, 64, 64], P('arch'), as said below
- coupling: float32 [40, 64, 128], P('arch'), may hold values from -0.75 to 0.75
- port_stiffness: float32 [40, 128, 128], P('arch'), as said below
- coupling_offset: float32 [8192, 64, 128], P(('inst', 'arch')), may hold values from -0.375 to 0.375
Outputs:
- assembled: float32 [16384, 7168], P(('inst', 'arch'))
Inputs may be any that keep to these rules, and one draw needn't show every extreme that they name: `instance_ports`: every port is named exactly twice: once at slot 0 and once at slot 1 of two different instances, or once at slot 2 and once at slot 3 of two different instances; an instance's four ports are distinct. `port_row`: A permutation of the ports. Among the 256 port slots of one device's instances, at most 3 name ports whose row lies in one device's (128) rows, and this many is reached. `bubble_inverse`: each matrix is symmetric. `port_stiffness`: each matrix is symmetric.
All inputs are finite; a program needn't handle non-finite values.
Results may differ from a plain program's by a relative error of at most 0.00013.
Values sent between devices are 32-bit elements; how exact they have to be, the bound alone decides.
A program may use at most 128 MiB of HBM per device.

v0:
```python
import jax
import jax.numpy as jnp
import numpy as np
from jax import lax
from jax.sharding import PartitionSpec as P


def orders(width):
    result = []
    for which in range(4):
        parts = [np.arange(which * width, (which + 1) * width)]
        for other in range(4):
            if other != which:
                parts.append(np.arange(other * width, (other + 1) * width))
        result.append(np.concatenate(parts))
    return result


def condense(inverses, couplings, stiffness, table, arch_ids, param_ids, offsets):
    scales = jnp.take(table, param_ids, axis=0)
    weighted = scales[:, :, None] * (jnp.take(couplings, arch_ids, axis=0) + offsets)
    applied = jnp.einsum(
        "bmn,bnq->bmq",
        jnp.take(inverses, arch_ids, axis=0),
        weighted,
        precision=lax.Precision.HIGHEST,
    )
    return jnp.take(stiffness, arch_ids, axis=0) - jnp.einsum(
        "bmp,bmq->bpq", weighted, applied, precision=lax.Precision.HIGHEST
    )


def body(
    instance_arch,
    instance_param,
    instance_ports,
    port_row,
    param_table,
    bubble_inverse,
    coupling,
    port_stiffness,
    coupling_offset,
):
    instances = instance_arch.shape[0]
    width = port_stiffness.shape[1] // 4
    flat_width = 4 * width * width
    inverses, couplings, stiffness = (
        lax.all_gather(bubble_inverse, "arch", axis=0, tiled=True),
        lax.all_gather(coupling, "arch", axis=0, tiled=True),
        lax.all_gather(port_stiffness, "arch", axis=0, tiled=True),
    )
    schur = condense(
        inverses, couplings, stiffness, param_table, instance_arch, instance_param, coupling_offset
    )
    columns = orders(width)
    strips = jnp.concatenate(
        [
            schur[:, which * width : (which + 1) * width, :][:, :, columns[which]]
            for which in range(4)
        ],
        axis=0,
    )
    strips = strips.reshape(4 * instances, flat_width)
    row_ids = jnp.take(port_row, instance_ports, axis=0).T.reshape(4 * instances)
    slot_ids = jnp.repeat(jnp.arange(4, dtype=jnp.int32), instances)
    row_codes = row_ids * 4 + slot_ids
    inst_count = lax.axis_size("inst")
    arch_count = lax.axis_size("arch")
    owners = inst_count * arch_count
    port_count = 2 * instances
    capacity = 4 * instances // owners * 3 // 2
    owner_ids = row_ids // port_count
    owner_hits = (owner_ids[:, None] == jnp.arange(owners, dtype=jnp.int32)[None, :]).astype(
        jnp.int32
    )
    ordinal = jnp.sum((jnp.cumsum(owner_hits, axis=0) - 1) * owner_hits, axis=1)
    buffer_slot = owner_ids * capacity + ordinal
    chosen = buffer_slot[None, :] == jnp.arange(owners * capacity, dtype=jnp.int32)[:, None]
    outgoing = jnp.dot(
        chosen.astype(jnp.float32),
        strips,
        precision=lax.Precision.HIGHEST,
        preferred_element_type=jnp.float32,
    )
    filled = jnp.any(chosen, axis=1)
    out_codes = jnp.where(filled, jnp.sum(jnp.where(chosen, row_codes[None, :], 0), axis=1), -1)
    incoming, in_codes = (
        lax.all_to_all(
            outgoing.reshape(owners, capacity, flat_width),
            ("inst", "arch"),
            split_axis=0,
            concat_axis=0,
            tiled=True,
        ),
        lax.all_to_all(
            out_codes.reshape(owners, capacity),
            ("inst", "arch"),
            split_axis=0,
            concat_axis=0,
            tiled=True,
        ),
    )
    incoming = incoming.reshape(owners * capacity, flat_width)
    in_codes = in_codes.reshape(owners * capacity)
    my_index = lax.axis_index("inst") * arch_count + lax.axis_index("arch")
    live_slot = in_codes >= 0
    local_row = jnp.where(live_slot, in_codes // 4 - my_index * port_count, port_count)
    parity = in_codes % 4 % 2
    even_index = jnp.where(live_slot & (parity == 0), local_row, port_count)
    odd_index = jnp.where(live_slot & (parity == 1), local_row, port_count)
    targets = jnp.arange(port_count, dtype=jnp.int32)[:, None]
    placing = jnp.concatenate(
        [
            local_row[None, :] == targets,
            even_index[None, :] == targets,
            odd_index[None, :] == targets,
        ],
        axis=0,
    )
    placed = jnp.dot(
        placing.astype(jnp.float32),
        incoming,
        precision=lax.Precision.HIGHEST,
        preferred_element_type=jnp.float32,
    )
    placed = placed.reshape(3, port_count, width, 4 * width)
    joined = jnp.concatenate(
        [placed[0, :, :, :width], placed[1, :, :, width:], placed[2, :, :, width:]], axis=2
    )
    return joined.reshape(port_count, 7 * width * width)


def solution(mesh):
    return jax.shard_map(
        body,
        mesh=mesh,
        in_specs=(
            P(("inst", "arch")),
            P(("inst", "arch")),
            P(("inst", "arch"), None),
            P(),
            P(),
            P("arch", None, None),
            P("arch", None, None),
            P("arch", None, None),
            P(("inst", "arch"), None, None),
        ),
        out_specs=P(("inst", "arch"), None),
        check_vma=False,
    )
```

profile of v0, /device:TPU:6, one launch (start us, length us, event | category | flops | bytes accessed | tf_op | source)
XLA Modules:
  0.0 307.8 jit_solution(5884704730045930546)
XLA Ops:
  6.5 0.7 all-gather.5.cloned.1.call-update
  7.3 0.7 all-gather.3.cloned.1.call-update
  8.0 0.7 compare_select_fusion
  8.7 0.1 copy.92
  8.8 0.1 reshape.302
  9.0 1.7 gather_fusion
  10.7 0.1 reshape.301
  11.0 0.1 copy.94
  11.1 0.2 fusion.9
  11.7 0.2 fusion.10
  11.8 0.2 fusion.4
  12.0 0.1 select_reduce_fusion
  12.2 0.8 select_n.162
  13.0 10.5 %all-to-all-start = ((s32[128,1,3]{2,1,0:T(1,128)}), s32[128,1,3]{2,1,0:T(1,128)S(1)}, u32[]{:S(2)}, u32[]{:S(2)}) async-start(s32[128,1,3]{2,1,0:T(1,128)} %bitcast.4), calls=%async_computation | async-start | bytes 131072 | tf_op jit(solution)/shard_map/all_to_all | solution.py:95
  23.5 0.2 copy.97
  23.7 0.6 gather_fusion.2
  24.4 22.8 %all_gather.11 = f32[40,64,64]{2,1,0:T(8,128)S(1)} all-gather(f32[10,64,64]{2,1,0:T(8,128)S(1)} %copy-done.3), channel_id=1, replica_groups=mesh['inst'=32,'arch'=4] {'arch'}, dimensions={0}, use_global_device_ids=true | all-gather | bytes 819200 | tf_op jit(solution)/shard_map/all_gather | solution.py:48
  47.2 2.0 gather_fusion.4
  49.4 2.0 gather_fusion.3
  51.4 6.2 %fusion = f32[64,64,128]{2,1,0:T(8,128)} fusion(f32[64,64,64]{2,1,0:T(8,128)} %gather_fusion.4, pred[64]{0:T(512)(128)(4,1)S(1)} %compare_and_fusion.1, f32[64,64,128]{2,1,0:T(8,128)} %param.25, f32[64,64,128]{2,1,0:T(8,128)S(1)} %gather_fusion.3, f32[64,64]{1,0:T(8,128)S(1)} %broadcast_select_fusion), kind=kOutput, calls=%fused_computation.12 | convolution fusion | flops 404488192 | bytes 7356480 | tf_op jit(solution)/shard_map/bmn,bnq->bmq/dot_general | solution.py:22
  57.6 22.4 %all-gather.3.cloned.1.call-done = f32[40,128,128]{2,1,0:T(8,128)} async-done(((f32[10,128,128]{2,1,0:T(8,128)}), f32[40,128,128]{2,1,0:T(8,128)}) %all-gather.3.cloned.1.call-update) | async-done | bytes 2621456 | tf_op jit(solution)/shard_map/all_gather | solution.py:50
  79.9 4.6 %gather_fusion.1 = f32[64,128,128]{2,1,0:T(8,128)} fusion(f32[40,128,128]{2,1,0:T(8,128)} %all-gather.3.cloned.1.call-done, s32[1024]{0:T(1024)S(1)} %pad_clamp_fusion.5), kind=kCustom, calls=%fused_computation.1 | custom fusion | bytes 8388864 | tf_op jit(solution)/shard_map/jit(_take)/gather | solution.py:28
  84.6 11.6 %select_subtract_fusion = f32[64,128,128]{2,1,0:T(8,128)S(1)} fusion(f32[64,128,128]{2,1,0:T(8,128)} %gather_fusion.1, f32[64,64,128]{2,1,0:T(8,128)} %fusion, pred[64]{0:T(512)(128)(4,1)S(1)} %compare_and_fusion.1, f32[64,64,128]{2,1,0:T(8,128)} %param.25, f32[64,64,128]{2,1,0:T(8,128)S(1)} %gather_fusion.3, f32[64,64]{1,0:T(8,128)S(1)} %broadcast_select_fusion), kind=kOutput, calls=%fused_computation.10 | convolution fusion | flops 808976384 | bytes 14696512 | tf_op jit(solution)/shard_map/bmp,bmq->bpq/dot_general | solution.py:28
  96.1 1.4 fusion.20
  97.6 3.1 %copy.98 = f32[64,32,128]{0,1,2:T(8,128)} copy(f32[64,32,128]{2,1,0:T(8,128)S(1)} %get-tuple-element.9) | data formatting | bytes 2097152 | tf_op jit(solution)/shard_map/slice | solution.py:58
  100.7 2.9 copy.101
  103.6 3.0 copy.100
  106.7 2.9 copy.99
  109.6 3.6 %gather_fusion.5 = f32[128,64,32]{1,2,0:T(8,128)} fusion(f32[64,32,128]{0,1,2:T(8,128)} %copy.98, s32[1024]{0:T(1024)S(1)} %pad_clamp_fusion.3), kind=kCustom, calls=%fused_computation.5 | custom fusion | bytes 2097664 | tf_op jit(solution)/shard_map/gather | solution.py:58
  113.2 3.6 %gather_fusion.8 = f32[128,64,32]{1,2,0:T(8,128)} fusion(f32[64,32,128]{0,1,2:T(8,128)} %copy.101, s32[1024]{0:T(1024)S(1)} %pad_clamp_fusion), kind=kCustom, calls=%fused_computation.8 | custom fusion | bytes 2097664 | tf_op jit(solution)/shard_map/gather | solution.py:58
  116.8 2.1 gather_fusion.7
  118.9 3.7 %gather_fusion.6 = f32[128,64,32]{1,2,0:T(8,128)} fusion(f32[64,32,128]{0,1,2:T(8,128)} %copy.99, s32[1024]{0:T(1024)S(1)} %pad_clamp_fusion.2), kind=kCustom, calls=%fused_computation.6 | custom fusion | bytes 2097664 | tf_op jit(solution)/shard_map/gather | solution.py:58
  122.6 6.6 %pad_maximum_fusion = f32[256,32,128]{0,1,2:T(8,128)} fusion(f32[64,32,128]{0,1,2:T(8,128)} %bitcast.39, f32[64,32,128]{0,1,2:T(8,128)} %bitcast.40, f32[64,32,128]{0,1,2:T(8,128)} %bitcast.41, f32[64,32,128]{0,1,2:T(8,128)S(1)} %bitcast.38), kind=kLoop, calls=%fused_computation.9 | loop fusion | flops 3145728 | bytes 8388608 | tf_op jit(solution)/shard_map/concatenate | solution.py:56
  129.2 5.9 %copy.102 = f32[256,32,128]{2,1,0:T(8,128)} copy(f32[256,32,128]{0,1,2:T(8,128)} %pad_maximum_fusion) | data formatting | bytes 8388608 | tf_op jit(solution)/shard_map/concatenate | solution.py:56
  135.1 5.0 %reshape.378 = f32[256,4096,1]{1,0,2:T(8,128)} reshape(f32[256,32,128]{2,1,0:T(8,128)} %copy.102) | data formatting | bytes 8388608 | tf_op jit(solution)/shard_map/reshape | solution.py:63
  140.1 4.8 %fusion.5 = f32[128,3,4096]{2,0,1:T(8,128)S(1)} fusion(f32[256,4096,1]{1,0,2:T(8,128)} %reshape.378, s32[128,3]{0,1:T(4,128)S(1)} %multiply_add_fusion, s32[256]{0:T(256)S(1)} %multiply_add_fusion.2), kind=kOutput, calls=%fused_computation.24 | convolution fusion | flops 4831936512 | bytes 10488320 | tf_op jit(solution)/shard_map/dot_general | solution.py:79
  144.9 7.5 %copy.103 = f32[128,3,4096]{2,1,0:T(4,128)} copy(f32[128,3,4096]{2,0,1:T(8,128)S(1)} %fusion.5) | data formatting | bytes 12582912 | tf_op jit(solution)/shard_map/dot_general | solution.py:79
  152.5 8.6 %all-to-all-start.1 = ((f32[128,3,4096]{2,1,0:T(4,128)}), f32[128,3,4096]{2,1,0:T(4,128)}, u32[]{:S(2)}, u32[]{:S(2)}) async-start(f32[128,3,4096]{2,1,0:T(4,128)} %copy.103), calls=%async_computation.1 | async-start | bytes 16777216 | tf_op jit(solution)/shard_map/all_to_all | solution.py:88
  161.1 0.5 broadcast.419
  161.6 0.8 reduce.3
  162.4 0.2 reshape.296
  162.8 106.3 %all-to-all-done.1 = f32[128,3,4096]{2,1,0:T(4,128)} async-done(((f32[128,3,4096]{2,1,0:T(4,128)}), f32[128,3,4096]{2,1,0:T(4,128)}, u32[]{:S(2)}, u32[]{:S(2)}) %all-to-all-start.1) | async-done | bytes 6291488 | tf_op jit(solution)/shard_map/all_to_all | solution.py:88
  269.1 9.5 %reshape.298 = f32[384,4096]{1,0:T(8,128)} reshape(f32[128,3,4096]{2,1,0:T(4,128)} %all-to-all-done.1) | data formatting | bytes 12582912 | tf_op jit(solution)/shard_map/reshape | solution.py:103
  278.6 6.6 %copy.104 = f32[4096,384]{1,0:T(8,128)} copy(f32[4096,384]{0,1:T(8,128)} %bitcast.36) | data formatting | bytes 12582912 | tf_op jit(solution)/shard_map/dot_general | solution.py:120
  285.2 8.1 %fusion.21 = f32[3,128,32,128]{1,3,2,0:T(8,128)S(1)} fusion(pred[3,128,384,1]{2,1,3,0:T(32,128)(4,1)S(1)} %bitcast.42, f32[32,128,384,1]{2,1,0,3:T(8,128)} %bitcast.35), kind=kOutput, calls=%fused_computation.86 | convolution fusion | flops 7247757312 | bytes 12730368 | tf_op jit(solution)/shard_map/dot_general | solution.py:120
  293.4 0.3 slice_bitcast_fusion.1
  293.7 2.0 pad_maximum_fusion.1
  295.7 5.3 %copy.105 = f32[128,7168]{1,0:T(8,128)} copy(f32[128,7168]{0,1:T(8,128)} %bitcast.37) | data formatting | bytes 7340032 | tf_op jit(solution)/shard_map/reshape | solution.py:130
  (61 shorter events, 0.9 us)
Async XLA Ops:
  6.5 2.4 copy-start
  6.5 42.8 %all-gather.5.cloned.1.call-start = ((), (), s32[]{:S(2)}) async-start(), calls=%async_computation.3 | async-start | bytes 1638400 | tf_op jit(solution)/shard_map/all_gather | solution.py:49
  7.3 72.7 %all-gather.3.cloned.1.call-start = ((), (), s32[]{:S(2)}) async-start(), calls=%async_computation.2 | async-start | bytes 3276800 | tf_op jit(solution)/shard_map/all_gather | solution.py:50
  8.9 2.0 copy-start.5
  8.9 14.6 %copy-start.4 = (f32[1024,64]{0,1:T(8,128)S(1)}, f32[1024,64]{0,1:T(8,128)}, u32[]{:S(2)}) copy-start(f32[1024,64]{0,1:T(8,128)} %param.21) | copy-start | bytes 786436
  8.9 14.8 %copy-start.10 = (s32[64]{0:T(128)S(1)}, s32[64]{0:T(128)}, u32[]{:S(2)}) copy-start(s32[64]{0:T(128)} %param.18) | copy-start | bytes 772
  10.7 13.6 %copy-start.9 = (s32[64]{0:T(128)S(1)}, s32[64]{0:T(128)}, u32[]{:S(2)}) copy-start(s32[64]{0:T(128)} %param.17) | copy-start | bytes 772
  10.7 13.7 %copy-start.3 = (f32[10,64,64]{2,1,0:T(8,128)S(1)}, f32[10,64,64]{2,1,0:T(8,128)}, u32[]{:S(2)}) copy-start(f32[10,64,64]{2,1,0:T(8,128)} %param.22) | copy-start | bytes 491524
  13.0 139.4 %all-to-all-start = ((s32[128,1,3]{2,1,0:T(1,128)}), s32[128,1,3]{2,1,0:T(1,128)S(1)}, u32[]{:S(2)}, u32[]{:S(2)}) async-start(s32[128,1,3]{2,1,0:T(1,128)} %bitcast.4), calls=%async_computation | async-start | bytes 131072 | tf_op jit(solution)/shard_map/all_to_all | solution.py:95
  47.2 2.0 copy-start.8
  47.2 2.0 copy-start.7
  47.2 2.1 copy-start.6
  118.9 3.7 %copy-start.2 = (f32[128,64,32]{1,2,0:T(8,128)S(1)}, f32[128,64,32]{1,2,0:T(8,128)}, u32[]{:S(2)}) copy-start(f32[128,64,32]{1,2,0:T(8,128)} %gather_fusion.5) | copy-start | bytes 3145732
  152.5 116.6 %all-to-all-start.1 = ((f32[128,3,4096]{2,1,0:T(4,128)}), f32[128,3,4096]{2,1,0:T(4,128)}, u32[]{:S(2)}, u32[]{:S(2)}) async-start(f32[128,3,4096]{2,1,0:T(4,128)} %copy.103), calls=%async_computation.1 | async-start | bytes 16777216 | tf_op jit(solution)/shard_map/all_to_all | solution.py:88
  295.7 5.3 %copy-start.1 = (s32[16384]{0:T(1024)S(1)}, s32[16384]{0:T(1024)}, u32[]{:S(2)}) copy-start(s32[16384]{0:T(1024)} %param.20) | copy-start | bytes 196612
Sparse Core Ops, SparseCore 0:
  9.0 33.6 all-gather.4
  44.4 35.4 all-gather.2
where the time goes:
time: 309 us; the launch traced here: 308 us
  waiting for transfers between devices  130 us (42%)
  local copies, waits for them, and re-layouts  80.1 us (26%)
  matrix products  30.7 us (10%)
  blocking collectives  22.8 us (7%)
  starting transfers between devices  19.1 us (6%)
  between operations  13.8 us (4%)
  other arithmetic  11.2 us (4%)
    all_to_all x1, waiting for transfers between devices, body(): lax.all_to_all(outgoing.reshape(owners, capacity, flat_width), ('inst', '...  106 us
    all_gather x1, blocking collectives, body(): lax.all_gather(bubble_inverse, 'arch', axis=0, tiled=True)  22.8 us
    all_gather x1, waiting for transfers between devices, body(): lax.all_gather(port_stiffness, 'arch', axis=0, tiled=True)  22.4 us
    slice x5, local copies, waits for them, and re-layouts, body(): schur[:, which * width:(which + 1) * width, :][:, :, columns[which]]  13.4 us
    gather x4, local copies, waits for them, and re-layouts, body(): schur[:, which * width:(which + 1) * width, :][:, :, columns[which]]  13 us
    dot_general x1, matrix products, condense(): jnp.einsum('bmp,bmq->bpq', weighted, applied, precision=lax.Precision.HIG...  11.6 us
    all_to_all x1, starting transfers between devices, body(): lax.all_to_all(out_codes.reshape(owners, capacity), ('inst', 'arch'), spl...  10.5 us
    reshape x1, local copies, waits for them, and re-layouts, body(): incoming = incoming.reshape(owners * capacity, flat_width)  9.5 us
  transfers between devices with their start and end apart: 4, of which 2 were waited for; matrix products, arithmetic and copies ran while one was open for 29% of the time, Pallas kernels for 0%

commit v1 on v0

--- a/solution.py
+++ b/solution.py
@@ -3,6 +3,11 @@
 import numpy as np
 from jax import lax
 from jax.sharding import PartitionSpec as P
+
+
+def exchange_gather(x, axis, along):
+    sent = jnp.stack([x] * lax.axis_size(axis))
+    return jnp.concatenate(lax.all_to_all(sent, axis, 0, 0), axis=along)
 
 
 def orders(width):
@@ -47,7 +52,7 @@
     inverses, couplings, stiffness = (
         lax.all_gather(bubble_inverse, "arch", axis=0, tiled=True),
         lax.all_gather(coupling, "arch", axis=0, tiled=True),
-        lax.all_gather(port_stiffness, "arch", axis=0, tiled=True),
+        exchange_gather(port_stiffness, "arch", 0),
     )
     schur = condense(
         inverses, couplings, stiffness, param_table, instance_arch, instance_param, coupling_offset

time: 309 us -> 316 us (1.023)
  blocking collectives: 22.8 us -> 49.3 us
  waiting for transfers between devices: 130 us -> 106 us
  starting transfers between devices: 19.1 us -> 23.8 us
  matrix products: 30.7 us -> 26.4 us
  local copies, waits for them, and re-layouts: 80.1 us -> 83.5 us
    all_gather x1, blocking collectives: 22.8 us -> 49.3 us  [body(): lax.all_gather(bubble_inverse, 'arch', axis=0, tiled=True)]
    all_gather x1 -> x0, waiting for transfers between devices: 22.4 us -> none  [body(): lax.all_gather(port_stiffness, 'arch', axis=0, tiled=True)]
    all_to_all x0 -> x1, starting transfers between devices: none -> 5.44 us  [exchange_gather(): return jnp.concatenate(lax.all_to_all(sent, axis, 0, 0), axis=along)]
    dot_general x1, matrix products: 11.6 us -> 8.33 us  [condense(): jnp.einsum('bmp,bmq->bpq', weighted, applied, precision=lax.Precision.HIG...]
  transfers between devices with their start and end apart: 4 -> 4, of which waited for: 2 -> 1; matrix products, arithmetic and copies ran while one was open for 29% -> 28% of each run, Pallas kernels for 0% -> 0%
where the time goes in v1:
time: 316 us; the launch traced here: 314 us
  waiting for transfers between devices  106 us (34%)
  local copies, waits for them, and re-layouts  83.5 us (26%)
  blocking collectives  49.3 us (16%)
  matrix products  26.4 us (8%)
  starting transfers between devices  23.8 us (8%)
  between operations  13.8 us (4%)
  other arithmetic  10.5 us (3%)
    all_to_all x1, waiting for transfers between devices, body(): lax.all_to_all(outgoing.reshape(owners, capacity, flat_width), ('inst', '...  106 us
    all_gather x1, blocking collectives, body(): lax.all_gather(bubble_inverse, 'arch', axis=0, tiled=True)  49.3 us
    slice x5, local copies, waits for them, and re-layouts, body(): schur[:, which * width:(which + 1) * width, :][:, :, columns[which]]  13.4 us
    gather x4, local copies, waits for them, and re-layouts, body(): schur[:, which * width:(which + 1) * width, :][:, :, columns[which]]  13 us
    all_to_all x1, starting transfers between devices, body(): lax.all_to_all(outgoing.reshape(owners, capacity, flat_width), ('inst', '...  10.2 us
    reshape x1, local copies, waits for them, and re-layouts, body(): incoming = incoming.reshape(owners * capacity, flat_width)  9.5 us
    dot_general x1, matrix products, condense(): jnp.einsum('bmp,bmq->bpq', weighted, applied, precision=lax.Precision.HIG...  8.33 us
    dot_general x1, matrix products, body(): jnp.dot(placing.astype(jnp.float32), incoming, precision=lax.Precision.HI...  8.14 us
  transfers between devices with their start and end apart: 4, of which 1 were waited for; matrix products, arithmetic and copies ran while one was open for 28% of the time, Pallas kernels for 0%

profile of v1, /device:TPU:6, one launch (start us, length us, event | category | flops | bytes accessed | tf_op | source)
XLA Modules:
  0.0 313.7 jit_solution(11881706867353487767)
XLA Ops:
  6.5 0.7 all-gather.2.cloned.1.call-update
  7.3 2.9 stack.2
  10.1 5.4 %all-to-all-start.1 = ((f32[4,10,128,128]{3,2,1,0:T(8,128)}), f32[4,10,128,128]{3,2,1,0:T(8,128)S(1)}, u32[]{:S(2)}, u32[]{:S(2)}) async-start(f32[4,10,128,128]{3,2,1,0:T(8,128)} %stack.2), calls=%async_computation.1 | async-start | bytes 5242880 | tf_op jit(solution)/shard_map/all_to_all | solution.py:10
  15.6 0.1 copy.92
  15.7 0.1 reshape.308
  15.8 1.7 gather_fusion
  17.6 0.1 reshape.307
  17.8 0.1 reshape.298
  18.0 0.1 copy.94
  18.2 0.2 fusion.9
  18.5 0.2 fusion.10
  18.7 0.2 fusion.4
  18.9 0.1 select_reduce_fusion
  19.1 0.8 select_n.162
  19.9 1.2 copy.97
  21.1 0.6 gather_fusion.2
  21.7 49.3 %all_gather.7 = f32[40,64,64]{2,1,0:T(8,128)} all-gather(f32[10,64,64]{2,1,0:T(8,128)S(1)} %copy-done.5), channel_id=1, replica_groups=mesh['inst'=32,'arch'=4] {'arch'}, dimensions={0}, use_global_device_ids=true | all-gather | bytes 819200 | tf_op jit(solution)/shard_map/all_gather | solution.py:53
  71.1 3.3 %gather_fusion.4 = f32[64,64,64]{2,1,0:T(8,128)} fusion(f32[40,64,64]{2,1,0:T(8,128)} %all_gather.7, s32[1024]{0:T(1024)S(1)} %pad_clamp_fusion.5), kind=kCustom, calls=%fused_computation.4 | custom fusion | bytes 2097408 | tf_op jit(solution)/shard_map/jit(_take)/gather | solution.py:29
  74.6 8.1 %all-to-all-start = ((s32[128,1,3]{2,1,0:T(1,128)}), s32[128,1,3]{2,1,0:T(1,128)S(1)}, u32[]{:S(2)}, u32[]{:S(2)}) async-start(s32[128,1,3]{2,1,0:T(1,128)} %bitcast.4), calls=%async_computation | async-start | bytes 131072 | tf_op jit(solution)/shard_map/all_to_all | solution.py:100
  82.7 2.8 gather_fusion.1
  85.5 2.0 gather_fusion.3
  87.6 4.9 %fusion = f32[64,64,128]{2,1,0:T(8,128)S(1)} fusion(f32[64,64,64]{2,1,0:T(8,128)} %gather_fusion.4, pred[64]{0:T(512)(128)(4,1)S(1)} %compare_and_fusion.1, f32[64,64,128]{2,1,0:T(8,128)} %param.25, f32[64,64,128]{2,1,0:T(8,128)S(1)} %gather_fusion.3, f32[64,64]{1,0:T(8,128)S(1)} %broadcast_select_fusion), kind=kOutput, calls=%fused_computation.12 | convolution fusion | flops 404488192 | bytes 7356480 | tf_op jit(solution)/shard_map/bmn,bnq->bmq/dot_general | solution.py:27
  92.5 8.3 %select_subtract_fusion = f32[64,128,128]{2,1,0:T(8,128)S(1)} fusion(f32[64,128,128]{2,1,0:T(8,128)S(1)} %copy-done.2, f32[64,64,128]{2,1,0:T(8,128)S(1)} %fusion, pred[64]{0:T(512)(128)(4,1)S(1)} %compare_and_fusion.1, f32[64,64,128]{2,1,0:T(8,128)S(1)} %copy-done.3, f32[64,64,128]{2,1,0:T(8,128)S(1)} %gather_fusion.3, f32[64,64]{1,0:T(8,128)S(1)} %broadcast_select_fusion), kind=kOutput, calls=%fused_computation.10 | convolution fusion | flops 808976384 | bytes 14696512 | tf_op jit(solution)/shard_map/bmp,bmq->bpq/dot_general | solution.py:33
  100.8 1.4 fusion.20
  102.3 3.1 %copy.98 = f32[64,32,128]{0,1,2:T(8,128)} copy(f32[64,32,128]{2,1,0:T(8,128)S(1)} %get-tuple-element.9) | data formatting | bytes 2097152 | tf_op jit(solution)/shard_map/slice | solution.py:63
  105.4 2.9 copy.101
  108.3 3.0 copy.100
  111.4 2.9 copy.99
  114.3 3.6 %gather_fusion.5 = f32[128,64,32]{1,2,0:T(8,128)} fusion(f32[64,32,128]{0,1,2:T(8,128)} %copy.98, s32[1024]{0:T(1024)S(1)} %pad_clamp_fusion.3), kind=kCustom, calls=%fused_computation.5 | custom fusion | bytes 2097664 | tf_op jit(solution)/shard_map/gather | solution.py:63
  117.9 3.6 %gather_fusion.8 = f32[128,64,32]{1,2,0:T(8,128)} fusion(f32[64,32,128]{0,1,2:T(8,128)} %copy.101, s32[1024]{0:T(1024)S(1)} %pad_clamp_fusion), kind=kCustom, calls=%fused_computation.8 | custom fusion | bytes 2097664 | tf_op jit(solution)/shard_map/gather | solution.py:63
  121.5 2.1 gather_fusion.7
  123.6 3.7 %gather_fusion.6 = f32[128,64,32]{1,2,0:T(8,128)} fusion(f32[64,32,128]{0,1,2:T(8,128)} %copy.99, s32[1024]{0:T(1024)S(1)} %pad_clamp_fusion.2), kind=kCustom, calls=%fused_computation.6 | custom fusion | bytes 2097664 | tf_op jit(solution)/shard_map/gather | solution.py:63
  127.3 6.6 %pad_maximum_fusion = f32[256,32,128]{0,1,2:T(8,128)} fusion(f32[64,32,128]{0,1,2:T(8,128)} %bitcast.41, f32[64,32,128]{0,1,2:T(8,128)} %bitcast.42, f32[64,32,128]{0,1,2:T(8,128)} %bitcast.43, f32[64,32,128]{0,1,2:T(8,128)S(1)} %bitcast.40), kind=kLoop, calls=%fused_computation.9 | loop fusion | flops 3145728 | bytes 8388608 | tf_op jit(solution)/shard_map/concatenate | solution.py:61
  133.9 5.9 %copy.102 = f32[256,32,128]{2,1,0:T(8,128)} copy(f32[256,32,128]{0,1,2:T(8,128)} %pad_maximum_fusion) | data formatting | bytes 8388608 | tf_op jit(solution)/shard_map/concatenate | solution.py:61
  139.9 5.0 %reshape.384 = f32[256,4096,1]{1,0,2:T(8,128)} reshape(f32[256,32,128]{2,1,0:T(8,128)} %copy.102) | data formatting | bytes 8388608 | tf_op jit(solution)/shard_map/reshape | solution.py:68
  144.8 5.0 %fusion.5 = f32[128,3,4096]{2,0,1:T(8,128)S(1)} fusion(f32[256,4096,1]{1,0,2:T(8,128)} %reshape.384, s32[128,3]{0,1:T(4,128)S(1)} %multiply_add_fusion, s32[256]{0:T(256)S(1)} %multiply_add_fusion.2), kind=kOutput, calls=%fused_computation.24 | convolution fusion | flops 4831936512 | bytes 10488320 | tf_op jit(solution)/shard_map/dot_general | solution.py:84
  149.9 7.5 %copy.103 = f32[128,3,4096]{2,1,0:T(4,128)} copy(f32[128,3,4096]{2,0,1:T(8,128)S(1)} %fusion.5) | data formatting | bytes 12582912 | tf_op jit(solution)/shard_map/dot_general | solution.py:84
  157.4 10.2 %all-to-all-start.2 = ((f32[128,3,4096]{2,1,0:T(4,128)}), f32[128,3,4096]{2,1,0:T(4,128)}, u32[]{:S(2)}, u32[]{:S(2)}) async-start(f32[128,3,4096]{2,1,0:T(4,128)} %copy.103), calls=%async_computation.2 | async-start | bytes 16777216 | tf_op jit(solution)/shard_map/all_to_all | solution.py:93
  167.7 0.5 broadcast.421
  168.2 0.8 reduce.3
  169.0 0.2 reshape.301
  169.4 105.6 %all-to-all-done.2 = f32[128,3,4096]{2,1,0:T(4,128)} async-done(((f32[128,3,4096]{2,1,0:T(4,128)}), f32[128,3,4096]{2,1,0:T(4,128)}, u32[]{:S(2)}, u32[]{:S(2)}) %all-to-all-start.2) | async-done | bytes 6291488 | tf_op jit(solution)/shard_map/all_to_all | solution.py:93
  275.0 9.5 %reshape.304 = f32[384,4096]{1,0:T(8,128)} reshape(f32[128,3,4096]{2,1,0:T(4,128)} %all-to-all-done.2) | data formatting | bytes 12582912 | tf_op jit(solution)/shard_map/reshape | solution.py:108
  284.5 6.6 %copy.104 = f32[4096,384]{1,0:T(8,128)} copy(f32[4096,384]{0,1:T(8,128)} %bitcast.37) | data formatting | bytes 12582912 | tf_op jit(solution)/shard_map/dot_general | solution.py:125
  291.1 8.1 %fusion.21 = f32[3,128,32,128]{1,3,2,0:T(8,128)S(1)} fusion(pred[3,128,384,1]{2,1,3,0:T(32,128)(4,1)S(1)} %bitcast.44, f32[32,128,384,1]{2,1,0,3:T(8,128)} %bitcast.36), kind=kOutput, calls=%fused_computation.86 | convolution fusion | flops 7247757312 | bytes 12730368 | tf_op jit(solution)/shard_map/dot_general | solution.py:125
  299.3 0.3 slice_bitcast_fusion.1
  299.6 2.0 pad_maximum_fusion.1
  301.6 5.3 %copy.105 = f32[128,7168]{1,0:T(8,128)} copy(f32[128,7168]{0,1:T(8,128)} %bitcast.39) | data formatting | bytes 7340032 | tf_op jit(solution)/shard_map/reshape | solution.py:135
  (63 shorter events, 0.8 us)
Async XLA Ops:
  6.5 9.3 %copy-start = (s32[16384]{0:T(1024)S(1)}, s32[16384]{0:T(1024)}, u32[]{:S(2)}) copy-start(s32[16384]{0:T(1024)} %param.20) | copy-start | bytes 196612
  6.5 79.0 %all-gather.2.cloned.1.call-start = ((), (), s32[]{:S(2)}) async-start(), calls=%async_computation.3 | async-start | bytes 1638400 | tf_op jit(solution)/shard_map/all_gather | solution.py:54
  10.1 5.4 %copy-start.6 = (s32[64,4]{0,1:T(4,128)S(1)}, s32[64,4]{0,1:T(4,128)}, u32[]{:S(2)}) copy-start(s32[64,4]{0,1:T(4,128)} %param.19) | copy-start | bytes 3076
  10.1 64.4 %all-to-all-start.1 = ((f32[4,10,128,128]{3,2,1,0:T(8,128)}), f32[4,10,128,128]{3,2,1,0:T(8,128)S(1)}, u32[]{:S(2)}, u32[]{:S(2)}) async-start(f32[4,10,128,128]{3,2,1,0:T(8,128)} %stack.2), calls=%async_computation.1 | async-start | bytes 5242880 | tf_op jit(solution)/shard_map/all_to_all | solution.py:10
  15.8 3.2 %copy-start.11 = (s32[64]{0:T(128)S(1)}, s32[64]{0:T(128)}, u32[]{:S(2)}) copy-start(s32[64]{0:T(128)} %param.18) | copy-start | bytes 772
  17.6 4.1 %copy-start.10 = (s32[64]{0:T(128)S(1)}, s32[64]{0:T(128)}, u32[]{:S(2)}) copy-start(s32[64]{0:T(128)} %param.17) | copy-start | bytes 772
  17.6 4.1 %copy-start.5 = (f32[10,64,64]{2,1,0:T(8,128)S(1)}, f32[10,64,64]{2,1,0:T(8,128)}, u32[]{:S(2)}) copy-start(f32[10,64,64]{2,1,0:T(8,128)} %param.22) | copy-start | bytes 491524
  71.0 3.4 %copy-start.9 = (s32[128]{0:T(128)S(1)}, s32[128]{0:T(128)}, u32[]{:S(2)}) copy-start(s32[128]{0:T(128)} %constant.168) | copy-start | bytes 1540
  71.1 3.4 %copy-start.8 = (s32[128]{0:T(128)S(1)}, s32[128]{0:T(128)}, u32[]{:S(2)}) copy-start(s32[128]{0:T(128)} %constant.169) | copy-start | bytes 1540
  71.1 3.4 %copy-start.7 = (s32[128]{0:T(128)S(1)}, s32[128]{0:T(128)}, u32[]{:S(2)}) copy-start(s32[128]{0:T(128)} %constant.170) | copy-start | bytes 1540
  74.6 82.8 %all-to-all-start = ((s32[128,1,3]{2,1,0:T(1,128)}), s32[128,1,3]{2,1,0:T(1,128)S(1)}, u32[]{:S(2)}, u32[]{:S(2)}) async-start(s32[128,1,3]{2,1,0:T(1,128)} %bitcast.4), calls=%async_computation | async-start | bytes 131072 | tf_op jit(solution)/shard_map/all_to_all | solution.py:100
  87.5 4.9 %copy-start.2 = (f32[64,128,128]{2,1,0:T(8,128)S(1)}, f32[64,128,128]{2,1,0:T(8,128)}, u32[]{:S(2)}) copy-start(f32[64,128,128]{2,1,0:T(8,128)} %gather_fusion.1) | copy-start | bytes 12582916
  87.6 4.9 %copy-start.3 = (f32[64,64,128]{2,1,0:T(8,128)S(1)}, f32[64,64,128]{2,1,0:T(8,128)}, u32[]{:S(2)}) copy-start(f32[64,64,128]{2,1,0:T(8,128)} %param.25) | copy-start | bytes 6291460
  123.6 3.7 %copy-start.4 = (f32[128,64,32]{1,2,0:T(8,128)S(1)}, f32[128,64,32]{1,2,0:T(8,128)}, u32[]{:S(2)}) copy-start(f32[128,64,32]{1,2,0:T(8,128)} %gather_fusion.5) | copy-start | bytes 3145732
  157.4 117.6 %all-to-all-start.2 = ((f32[128,3,4096]{2,1,0:T(4,128)}), f32[128,3,4096]{2,1,0:T(4,128)}, u32[]{:S(2)}, u32[]{:S(2)}) async-start(f32[128,3,4096]{2,1,0:T(4,128)} %copy.103), calls=%async_computation.2 | async-start | bytes 16777216 | tf_op jit(solution)/shard_map/all_to_all | solution.py:93
  301.6 5.3 %copy-start.1 = (s32[16384]{0:T(1024)S(1)}, s32[16384]{0:T(1024)}, u32[]{:S(2)}) copy-start(s32[16384]{0:T(1024)} %param.20) | copy-start | bytes 196612
Sparse Core Ops, SparseCore 0:
  9.0 51.6 all-gather.1
